TPU v7x, 512 devices: a whole 4x8x8 slice. The times are simulated.
512 devices in a mesh: row: 32 (over y, z_lo, core), col: 16 (over x, z_hi).
Axes of the slice: x: 4, y: 8, z: 8 (z_hi: 4, z_lo: 2; z = z_hi * 2 + z_lo), core: 2. Of those that a mesh axis runs over, the one named last changes fastest.
Arguments:
- features: bfloat16 [32768, 256], P(('row', 'col')), may hold values from -6 to 6
- grad_out: bfloat16 [32768, 256], P(('row', 'col')), may hold values from -6 to 6
- relu_mask: int32 [32768, 256], P(('row', 'col')), may hold values 0 or 1
- degree: int32 [32768], P(('row', 'col')), may hold values from 1 to 16
- weight: bfloat16 [256, 256], replicated, may hold values from -0.375 to 0.375
- adjacency: bfloat16 [32, 16, 96, 128, 128], P('row', 'col'), may hold values from -0.0625 to 0.0625
- block_slot: int32 [32, 16, 96], P('row', 'col'), may hold values from 0 to 127, as said below
- block_count: int32 [32, 16], P('row', 'col'), may hold values from 1 to 96, as said below
Outputs:
- grad_features: float32 [32768, 256], P(('row', 'col'))
- weight_grad: float32 [256, 256], replicated
Inputs may be any that keep to these rules, and one draw needn't show every extreme that they name: `block_slot`: within one tile the positions are distinct. `block_count`: some tile uses all 96 entries.
All inputs are finite; a program needn't handle non-finite values. No bound on the sum of `relu_mask` on one device may be relied on, other than what follows from the above.
Results may differ from a plain program's by a relative error of at most 0.0075.
Values may be sent and summed in bfloat16 or wider, within the bound.
A program may use at most 64 MiB of HBM per device.

v0:
```python
import math

import jax
import jax.numpy as jnp
from jax import lax
from jax.sharding import PartitionSpec as P


def block_pass(tile_blocks, source_ids, target_ids, live_count, source, target_count, transpose):
    slot_count = tile_blocks.shape[0]
    block_size = tile_blocks.shape[-1]
    feature_width = source.shape[1]
    per_turn = math.gcd(slot_count, 16)
    turn_count = slot_count // per_turn
    pieces = source.reshape(-1, block_size, feature_width)
    einsum_form = "gab,gaf->gbf" if transpose else "gab,gbf->gaf"

    def advance(running, turn_index):
        offset = turn_index * per_turn
        group_blocks = lax.dynamic_slice_in_dim(tile_blocks, offset, per_turn, 0)
        group_source = lax.dynamic_slice_in_dim(source_ids, offset, per_turn, 0)
        group_target = lax.dynamic_slice_in_dim(target_ids, offset, per_turn, 0)
        live_mask = (offset + jnp.arange(per_turn) < live_count).astype(jnp.float32)
        picked = pieces[group_source]
        products = jnp.einsum(einsum_form, group_blocks, picked, preferred_element_type=jnp.float32)
        products = products * live_mask[:, None, None]
        running = running.at[group_target].add(products)
        return (running, None)

    running, unused = lax.scan(
        advance,
        jnp.zeros((target_count, block_size, feature_width), jnp.float32),
        jnp.arange(turn_count),
    )
    return running.reshape(target_count * block_size, feature_width)


def local(features, grad_out, relu_mask, degree, weight, adjacency, block_slot, block_count):
    own_rows = features.shape[0]
    row_devices = lax.axis_size("row")
    col_devices = lax.axis_size("col")
    block_size = adjacency.shape[-1]
    row_blocks = own_rows * col_devices // block_size
    col_blocks = own_rows * row_devices // block_size
    node_scale = lax.rsqrt(degree.astype(jnp.float32))[:, None]
    masked = grad_out * relu_mask.astype(jnp.bfloat16)
    scaled_grad = (masked.astype(jnp.float32) * node_scale).astype(jnp.bfloat16)
    tile_blocks = adjacency[0, 0]
    slots = block_slot[0, 0]
    live_count = block_count[0, 0]
    block_row = slots // col_blocks
    block_col = slots % col_blocks
    grad_rows = lax.all_gather(scaled_grad, "col", axis=0, tiled=True)
    partial_value = block_pass(
        tile_blocks, block_row, block_col, live_count, grad_rows, col_blocks, True
    )
    summed = lax.psum_scatter(partial_value, "row", scatter_dimension=0, tiled=True)
    pulled = summed * node_scale
    grad_features = jnp.dot(pulled, weight.astype(jnp.float32).T, precision=lax.Precision.HIGHEST)
    scaled_feat = (features.astype(jnp.float32) * node_scale).astype(jnp.bfloat16)
    feat_cols = lax.all_gather(scaled_feat, "row", axis=0, tiled=True)
    forward = block_pass(
        tile_blocks, block_col, block_row, live_count, feat_cols, row_blocks, False
    )
    aggregated = lax.psum_scatter(forward, "col", scatter_dimension=0, tiled=True) * node_scale
    local_grad = jnp.dot(aggregated.T, masked.astype(jnp.float32), precision=lax.Precision.HIGHEST)
    node_total = own_rows * row_devices * col_devices
    weight_grad = lax.psum(local_grad, ("row", "col")) * node_total ** (-0.5)
    return (grad_features, weight_grad)


def solution(mesh):
    placed = (
        P(("row", "col"), None),
        P(("row", "col"), None),
        P(("row", "col"), None),
        P(("row", "col")),
        P(),
        P("row", "col", None, None, None),
        P("row", "col", None),
        P("row", "col"),
    )
    return jax.shard_map(
        local, mesh=mesh, in_specs=placed, out_specs=(P(("row", "col"), None), P()), check_vma=False
    )
```

profile of v0, /device:TPU:1, one launch (start us, length us, event | category | flops | bytes accessed | tf_op | source)
XLA Modules:
  0.0 630.0 jit_solution(6121418989717779897)
XLA Ops:
  10.2 48.9 %all_gather.6 = bf16[1024,256]{1,0:T(8,128)(2,1)} all-gather(bf16[64,256]{1,0:T(8,128)(2,1)S(1)} %get-tuple-element.133), channel_id=1, replica_groups=mesh['row'=32,'col'=16] {'col'}, dimensions={0}, use_global_device_ids=true | all-gather | bytes 557056 | tf_op jit(solution)/shard_map/all_gather | solution.py:53
  59.1 23.8 %all-gather.2.cloned.1.call-done = bf16[2048,256]{1,0:T(8,128)(2,1)} async-done(((bf16[64,256]{1,0:T(8,128)(2,1)}), bf16[2048,256]{1,0:T(8,128)(2,1)}) %all-gather.2.cloned.1.call-update) | async-done | bytes 1048592 | tf_op jit(solution)/shard_map/all_gather | solution.py:61
  83.0 53.4 %while.21 = (s32[]{:T(128)}, f32[8,128,256]{2,1,0:T(8,128)S(1)}, s32[6]{0:T(128)S(1)}, s32[96]{0:T(128)S(1)}, bf16[96,128,128]{2,1,0:T(8,128)(2,1)}, /*index=5*/...) while((s32[]{:T(128)}, f32[8,128,256]{2,1,0:T(8,128)S(1)}, ...), condition=%wide.region_6.7_spmd, body=%wide.region_4.6_spmd.sunk | while | flops 135267472 | bytes 12063487 | solution.py:30
  84.4 2.9 gather_fusion.1
  93.3 2.9 gather_fusion.1
  98.6 2.2 scatter_fusion.1
  102.1 2.9 gather_fusion.1
  107.5 2.2 scatter_fusion.1
  111.0 2.9 gather_fusion.1
  116.4 2.2 scatter_fusion.1
  119.9 2.9 gather_fusion.1
  125.3 2.2 scatter_fusion.1
  128.8 2.9 gather_fusion.1
  134.2 2.2 scatter_fusion.1
  139.0 57.6 %while.20 = (s32[]{:T(128)}, f32[16,128,256]{2,1,0:T(8,128)}, s32[6]{0:T(128)S(1)}, s32[96]{0:T(128)S(1)}, bf16[96,128,128]{2,1,0:T(8,128)(2,1)}, /*index=5*/s32...) while((s32[]{:T(128)}, f32[16,128,256]{2,1,0:T(8,128)}, ...), condition=%wide.region_2.3_spmd, body=%wide.region_0.2_spmd.sunk | while | flops 135267472 | bytes 12063487 | solution.py:30
  144.2 4.3 scatter_fusion
  153.8 4.4 scatter_fusion
  163.4 4.4 scatter_fusion
  173.0 4.5 scatter_fusion
  182.6 4.5 scatter_fusion
  192.3 4.3 scatter_fusion
  196.7 30.8 %reduce-scatter.5.cloned.1.call-done = f32[64,256]{1,0:T(8,128)} async-done(((f32[1024,256]{1,0:T(8,128)}), f32[64,256]{1,0:T(8,128)}) %reduce-scatter.5.cloned.1.call-update) | async-done | bytes 65552 | tf_op jit(solution)/shard_map/reduce_scatter | solution.py:65
  229.5 118.2 %reduce-scatter.3.cloned.1.call-done = f32[64,256]{1,0:T(8,128)} async-done(((f32[2048,256]{1,0:T(8,128)}), f32[64,256]{1,0:T(8,128)}) %reduce-scatter.3.cloned.1.call-update) | async-done | bytes 65552 | tf_op jit(solution)/shard_map/reduce_scatter | solution.py:57
  349.5 272.3 %all-reduce.2.cloned.1.call-done = f32[256,256]{1,0:T(8,128)} async-done(((f32[256,256]{1,0:T(8,128)}), f32[256,256]{1,0:T(8,128)}) %all-reduce.2.cloned.1.call-update) | async-done | bytes 262160 | tf_op jit(solution)/shard_map/psum | solution.py:68
  (93 shorter events, 59.3 us)
Async XLA Ops:
  7.2 340.5 %copy-start = (bf16[256,256]{1,0:T(8,128)(2,1)S(1)}, bf16[256,256]{1,0:T(8,128)(2,1)}, u32[]{:S(2)}) copy-start(bf16[256,256]{1,0:T(8,128)(2,1)} %param.16) | copy-start | bytes 393220
  7.2 75.7 %all-gather.2.cloned.1.call-start = ((), (), s32[]{:S(2)}) async-start(), calls=%async_computation.3 | async-start | bytes 1081344 | tf_op jit(solution)/shard_map/all_gather | solution.py:61
  9.5 218.0 %reduce-scatter.5.cloned.1.call-start = ((), (), s32[]{:S(2)}) async-start(), calls=%async_computation.4 | async-start | bytes 1114112 | tf_op jit(solution)/shard_map/reduce_scatter | solution.py:65
  136.4 1.0 copy-start.1
  137.4 210.3 %reduce-scatter.3.cloned.1.call-start = ((), (), s32[]{:S(2)}) async-start(), calls=%async_computation.2 | async-start | bytes 2162688 | tf_op jit(solution)/shard_map/reduce_scatter | solution.py:57
  196.7 30.9 %copy-start.2 = (s32[64,256]{1,0:T(8,128)S(1)}, s32[64,256]{1,0:T(8,128)}, u32[]{:S(2)}) copy-start(s32[64,256]{1,0:T(8,128)} %param.14) | copy-start | bytes 196612
  196.7 30.9 %copy-start.3 = (bf16[64,256]{1,0:T(8,128)(2,1)S(1)}, bf16[64,256]{1,0:T(8,128)(2,1)}, u32[]{:S(2)}) copy-start(bf16[64,256]{1,0:T(8,128)(2,1)} %param.13) | copy-start | bytes 98308
  196.7 425.1 %all-reduce.2.cloned.1.call-start = ((), (), s32[]{:S(2)}) async-start(), calls=%async_computation.5 | async-start | bytes 524288 | tf_op jit(solution)/shard_map/psum | solution.py:68
Sparse Core Ops, SparseCore 0:
  10.7 72.1 all-gather.1
  137.5 89.9 reduce-scatter.4
  230.6 117.0 reduce-scatter.2
  353.1 268.5 all-reduce.1
where the time goes:
time: 632 us; the launch traced here: 630 us
  waiting for transfers between devices  445 us (70%)
  other arithmetic  53.1 us (8%)
  blocking collectives  48.9 us (8%)
  local copies, waits for them, and re-layouts  36.8 us (6%)
  matrix products  23.8 us (4%)
  between operations  13.8 us (2%)
  loops' own time  8.26 us (1%)
    psum x1, waiting for transfers between devices, local(): weight_grad = lax.psum(local_grad, ('row', 'col')) * node_total ** (-0.5)  272 us
    reduce_scatter x1, waiting for transfers between devices, local(): lax.psum_scatter(partial_value, 'row', scatter_dimension=0, tiled=True)  118 us
    all_gather x1, blocking collectives, local(): grad_rows = lax.all_gather(scaled_grad, 'col', axis=0, tiled=True)  48.9 us
    scatter-add x12, other arithmetic, advance(): running = running.at[group_target].add(products)  39.6 us
    reduce_scatter x1, waiting for transfers between devices, local(): lax.psum_scatter(forward, 'col', scatter_dimension=0, tiled=True)  30.8 us
    gather x12, local copies, waits for them, and re-layouts, advance(): picked = pieces[group_source]  27.1 us
    all_gather x1, waiting for transfers between devices, local(): feat_cols = lax.all_gather(scaled_feat, 'row', axis=0, tiled=True)  23.8 us
    dot_general x12, matrix products, advance(): jnp.einsum(einsum_form, group_blocks, picked, preferred_element_type=jnp....  20.1 us
  transfers between devices with their start and end apart: 4, of which 4 were waited for; matrix products, arithmetic and copies ran while one was open for 9% of the time, Pallas kernels for 0%

commit v1 on v0

v1 whole, which is shorter than its diff:
```python
import functools

import jax
import jax.numpy as jnp
from jax import lax
from jax.experimental import pallas as pl
from jax.experimental.pallas import tpu as pltpu
from jax.sharding import PartitionSpec as P

MESH = pl.DeviceIdType.MESH
BF = jnp.bfloat16
F32 = jnp.float32


def kernel(
    R, C, norm,
    feat_ref, gout_ref, mask_ref, deg_ref, w_ref, adj_hbm, slot_ref, count_ref,
    gf_ref, wg_ref,
    adj_v, a_dense, inv_v, inv_s, gbuf, gt, pall,
    s1_send, s1_recv, s2_send, s2_recv, s3_send, s3_recv, own,
    wpart, ra, wb, rb, rc,
    adj_sem, inv_sem, g_ss, g_rs, s1_ss, s1_rs, s2_ss, s2_rs, s3_ss, s3_rs,
    a_ss, a_rs, b_ss, b_rs, c_ss, c_rs, d_ss, d_rs, e_ss, e_rs,
):
    NY = R // 4
    M = R // 2
    entries, blk = adj_hbm.shape[0], adj_hbm.shape[1]
    width = feat_ref.shape[1]
    row = lax.axis_index("row")
    col = lax.axis_index("col")
    y = row // 4
    z = (row // 2) % 2
    c = row % 2
    m = row // 2
    sib = m * 2 + (1 - c)
    zrow = y * 4 + (1 - z) * 2 + c

    def rcopy(src, dst, ss, rs, dev):
        return pltpu.make_async_remote_copy(
            src_ref=src, dst_ref=dst, send_sem=ss, recv_sem=rs,
            device_id=dev, device_id_type=MESH,
        )

    adj_copy = pltpu.make_async_copy(adj_hbm, adj_v.at[pl.ds(0, entries)], adj_sem)
    adj_copy.start()

    bar = pltpu.get_barrier_semaphore()

    def greet_col(t, u):
        pl.semaphore_signal(bar, inc=1, device_id=(row, (col + t) % C), device_id_type=MESH)
        return u

    def greet_row(t, u):
        pl.semaphore_signal(bar, inc=1, device_id=(((m + t) % M) * 2 + c, col), device_id_type=MESH)
        return u

    lax.fori_loop(1, C, greet_col, 0)
    lax.fori_loop(1, M, greet_row, 0)
    pl.semaphore_signal(bar, inc=1, device_id=(sib, col), device_id_type=MESH)

    n = feat_ref.shape[0]
    scale_row = lax.rsqrt(deg_ref[...].astype(F32))
    eye = lax.broadcasted_iota(jnp.int32, (n, n), 0) == lax.broadcasted_iota(jnp.int32, (n, n), 1)
    scale = jnp.sum(jnp.where(eye, jnp.broadcast_to(scale_row, (n, n)), 0.0), axis=1, keepdims=True)
    masked = gout_ref[...].astype(F32) * mask_ref[...].astype(F32)
    gbuf[col] = (masked * scale).astype(BF)

    pl.semaphore_wait(bar, C - 1 + M - 1 + 1)

    def g_send(t, u):
        peer = (col + t) % C
        rcopy(gbuf.at[col], gbuf.at[col], g_ss.at[t], g_rs.at[col], (row, peer)).start()
        return u

    lax.fori_loop(1, C, g_send, 0)

    lane = lax.broadcasted_iota(jnp.int32, (8, 128), 1)
    live = count_ref[0, 0]

    def invert(b, acc):
        s = jnp.where(b < live, slot_ref[0, b], -1)
        return jnp.where(lane == s, b, acc)

    inv_v[...] = lax.fori_loop(0, entries, invert, jnp.full((8, 128), entries, jnp.int32))
    inv_copy = pltpu.make_async_copy(inv_v, inv_s, inv_sem)
    inv_copy.start()
    adj_v[entries] = jnp.zeros((blk, blk), BF)
    inv_copy.wait()
    adj_copy.wait()

    row_blocks = C * n // blk

    def fill(k, u):
        r = k // NY
        q = k % NY
        for h in range(2):
            e = inv_s[0, r * (2 * NY) + q * 2 + h]
            a_dense[q, pl.ds(pl.multiple_of(r * blk, blk), blk), pl.ds(h * blk, blk)] = adj_v[e]
        return u

    lax.fori_loop(0, row_blocks * NY, fill, 0)

    def g_wait(t, u):
        peer = (col + t) % C
        rcopy(gbuf.at[peer], gbuf.at[peer], g_ss.at[t], g_rs.at[peer], (row, peer)).wait()
        return u

    lax.fori_loop(1, C, g_wait, 0)

    def turn(k, u):
        piece = gbuf[pl.ds(2 * k, 2)].reshape(2 * n, width).astype(F32)
        gt[k] = piece.T.astype(BF)
        return u

    lax.fori_loop(0, C // 2, turn, 0)
    gtv = jnp.concatenate([gt[k] for k in range(C // 2)], axis=1)

    def product(t, u):
        q = (y + 1 + t) % NY
        pt = jnp.dot(gtv, a_dense[q], preferred_element_type=F32)
        pall[q] = pt.T.reshape(4, n, width)
        for zz in range(2):
            s1_send[q, zz] = pall[q, 2 * zz + 1 - c].astype(BF)
        rcopy(s1_send.at[q], s1_recv.at[q], s1_ss.at[q], s1_rs.at[q], (sib, col)).start()
        return u

    lax.fori_loop(0, NY, product, 0)

    def stage2(t, u):
        q = (y + 1 + t) % NY
        rcopy(s1_send.at[q], s1_recv.at[q], s1_ss.at[q], s1_rs.at[q], (sib, col)).wait()
        s2_send[q] = (pall[q, 2 * (1 - z) + c] + s1_recv[q, 1 - z].astype(F32)).astype(BF)
        rcopy(s2_send.at[q], s2_recv.at[q], s2_ss.at[q], s2_rs.at[q], (zrow, col)).start()
        return u

    lax.fori_loop(0, NY, stage2, 0)

    def total3(q):
        rcopy(s2_send.at[q], s2_recv.at[q], s2_ss.at[q], s2_rs.at[q], (zrow, col)).wait()
        return pall[q, 2 * z + c] + s1_recv[q, z].astype(F32) + s2_recv[q].astype(F32)

    def stage3(t, u):
        q = (y + 1 + t) % NY
        s3_send[q] = total3(q).astype(BF)
        rcopy(s3_send.at[q], s3_recv.at[y], s3_ss.at[q], s3_rs.at[y], (q * 4 + z * 2 + c, col)).start()
        return u

    lax.fori_loop(0, NY - 1, stage3, 0)
    own[...] = total3(y)

    def collect(t, u):
        q = (y + 1 + t) % NY
        rcopy(s3_send.at[q], s3_recv.at[q], s3_ss.at[q], s3_rs.at[q], (q * 4 + z * 2 + c, col)).wait()
        own[...] += s3_recv[q].astype(F32)
        return u

    lax.fori_loop(0, NY - 1, collect, 0)

    raw = own[...]
    sfeat = (feat_ref[...].astype(F32) * scale).astype(BF)
    raw_hi = raw.astype(BF)
    raw_lo = (raw - raw_hi.astype(F32)).astype(BF)
    over_nodes = (((0,), (0,)), ((), ()))
    wl = lax.dot_general(sfeat, raw_hi, over_nodes, preferred_element_type=F32)
    wl = wl + lax.dot_general(sfeat, raw_lo, over_nodes, preferred_element_type=F32)
    wpart[...] = wl.reshape(wpart.shape)

    rcopy(wpart.at[1 - c], ra, a_ss, a_rs, (sib, col)).start()

    pulled = raw * scale
    p_hi = pulled.astype(BF)
    p_lo = (pulled - p_hi.astype(F32)).astype(BF)
    over_last = (((1,), (1,)), ((), ()))
    w = w_ref[...]
    gf_ref[...] = lax.dot_general(p_hi, w, over_last, preferred_element_type=F32) + lax.dot_general(
        p_lo, w, over_last, preferred_element_type=F32
    )

    rcopy(wpart.at[1 - c], ra, a_ss, a_rs, (sib, col)).wait()
    wb[...] = wpart[c] + ra[...]

    def b_send(t, u):
        peer = (m + t) % M
        rcopy(wb.at[peer], rb.at[m], b_ss.at[t], b_rs.at[m], (peer * 2 + c, col)).start()
        return u

    lax.fori_loop(1, M, b_send, 0)
    rb[m] = wb[m]

    def b_wait(t, u):
        peer = (m + t) % M
        rcopy(wb.at[peer], rb.at[peer], b_ss.at[t], b_rs.at[peer], (peer * 2 + c, col)).wait()
        return u

    lax.fori_loop(1, M, b_wait, 0)
    rc[col] = jnp.sum(rb[...], axis=0)

    def c_send(t, u):
        peer = (col + t) % C
        rcopy(rc.at[col], rc.at[col], c_ss.at[t], c_rs.at[col], (row, peer)).start()
        return u

    lax.fori_loop(1, C, c_send, 0)

    def c_wait(t, u):
        peer = (col + t) % C
        rcopy(rc.at[peer], rc.at[peer], c_ss.at[t], c_rs.at[peer], (row, peer)).wait()
        return u

    lax.fori_loop(1, C, c_wait, 0)
    wg_ref[c, m] = jnp.sum(rc[...], axis=0) * norm

    def d_send(t, u):
        peer = (m + t) % M
        rcopy(wg_ref.at[c, m], wg_ref.at[c, m], d_ss.at[t], d_rs.at[m], (peer * 2 + c, col)).start()
        return u

    lax.fori_loop(1, M, d_send, 0)

    def d_wait(t, u):
        peer = (m + t) % M
        rcopy(wg_ref.at[c, peer], wg_ref.at[c, peer], d_ss.at[t], d_rs.at[peer], (peer * 2 + c, col)).wait()
        return u

    lax.fori_loop(1, M, d_wait, 0)
    rcopy(wg_ref.at[c], wg_ref.at[c], e_ss, e_rs, (sib, col)).start()
    rcopy(wg_ref.at[1 - c], wg_ref.at[1 - c], e_ss, e_rs, (sib, col)).wait()


def local(features, grad_out, relu_mask, degree, weight, adjacency, block_slot, block_count):
    R = lax.axis_size("row")
    C = lax.axis_size("col")
    n, width = features.shape
    entries, blk = adjacency.shape[2], adjacency.shape[3]
    NY, M = R // 4, R // 2
    part = (2, M, width // R, width)
    dma = pltpu.SemaphoreType.DMA
    vm = pltpu.VMEM
    vspec = pl.BlockSpec(memory_space=pltpu.VMEM)
    sspec = pl.BlockSpec(memory_space=pltpu.SMEM)
    gf, wg = pl.pallas_call(
        functools.partial(kernel, R, C, float((n * R * C) ** -0.5)),
        out_shape=(
            jax.ShapeDtypeStruct((n, width), F32),
            jax.ShapeDtypeStruct(part, F32),
        ),
        in_specs=[vspec] * 5 + [pl.BlockSpec(memory_space=pl.ANY), sspec, sspec],
        out_specs=(vspec, vspec),
        scratch_shapes=[
            vm((entries + 1, blk, blk), BF),
            vm((NY, C * n, 2 * blk), BF),
            vm((8, 128), jnp.int32),
            pltpu.SMEM((8, 128), jnp.int32),
            vm((C, n, width), BF),
            vm((C // 2, width, 2 * n), BF),
            vm((NY, 4, n, width), F32),
            vm((NY, 2, n, width), BF),
            vm((NY, 2, n, width), BF),
            vm((NY, n, width), BF),
            vm((NY, n, width), BF),
            vm((NY, n, width), BF),
            vm((NY, n, width), BF),
            vm((n, width), F32),
            vm(part, F32),
            vm(part[1:], F32),
            vm(part[1:], F32),
            vm(part[1:], F32),
            vm((C,) + part[2:], F32),
            dma, dma,
            dma((C,)), dma((C,)),
            dma((NY,)), dma((NY,)),
            dma((NY,)), dma((NY,)),
            dma((NY,)), dma((NY,)),
            dma, dma,
            dma((M,)), dma((M,)),
            dma((C,)), dma((C,)),
            dma((M,)), dma((M,)),
            dma, dma,
        ],
        compiler_params=pltpu.CompilerParams(
            collective_id=0, has_side_effects=True, vmem_limit_bytes=56 * 1024 * 1024
        ),
    )(
        features, grad_out, relu_mask, degree.reshape(1, n), weight,
        adjacency.reshape(entries, blk, blk), block_slot.reshape(1, entries), block_count,
    )
    return gf, wg.reshape(width, width)


def solution(mesh):
    placed = (
        P(("row", "col"), None),
        P(("row", "col"), None),
        P(("row", "col"), None),
        P(("row", "col")),
        P(),
        P("row", "col", None, None, None),
        P("row", "col", None),
        P("row", "col"),
    )
    return jax.shard_map(
        local, mesh=mesh, in_specs=placed, out_specs=(P(("row", "col"), None), P()), check_vma=False
    )
```

time: 632 us -> 77.9 us (0.12)
  waiting for transfers between devices: 445 us -> 0 us
  Pallas kernels: 0 us -> 73.3 us
  other arithmetic: 53.1 us -> 0 us
  blocking collectives: 48.9 us -> 0 us
  local copies, waits for them, and re-layouts: 36.8 us -> 3.14 us
  matrix products: 23.8 us -> 0 us
  between operations: 13.8 us -> 1.29 us
  loops' own time: 8.26 us -> 0 us
    psum x1 -> x0, waiting for transfers between devices: 272 us -> none  [local(): weight_grad = lax.psum(local_grad, ('row', 'col')) * node_total ** (-0.5)]
    reduce_scatter x2 -> x0, waiting for transfers between devices: 149 us -> none  [the longest x1 118 us: local(): lax.psum_scatter(partial_value, 'row', scatter_dimension=0, tiled=True)]
    pallas_call x0 -> x1, Pallas kernels: none -> 73.3 us  [local(): pl.pallas_call(functools.partial(kernel, R, C, float((n * R * C) ** (-0.5...]
    all_gather x1 -> x0, blocking collectives: 48.9 us -> none  [local(): grad_rows = lax.all_gather(scaled_grad, 'col', axis=0, tiled=True)]
    scatter-add x12 -> x0, other arithmetic: 39.6 us -> none  [advance(): running = running.at[group_target].add(products)]
    gather x12 -> x0, local copies, waits for them, and re-layouts: 27.1 us -> none  [advance(): picked = pieces[group_source]]
    all_gather x1 -> x0, waiting for transfers between devices: 23.8 us -> none  [local(): feat_cols = lax.all_gather(scaled_feat, 'row', axis=0, tiled=True)]
    dot_general x14 -> x0, matrix products: 23.8 us -> none  [the longest x12 20.1 us: advance(): jnp.einsum(einsum_form, group_blocks, picked, preferred_element_type=jnp....]
  transfers between devices with their start and end apart: 4 -> 0, of which waited for: 4 -> 0; matrix products, arithmetic and copies ran while one was open for 9% -> 0% of each run, Pallas kernels for 0% -> 0%
where the time goes in v1:
time: 77.9 us; the launch traced here: 77.7 us
  Pallas kernels  73.3 us (94%)
  local copies, waits for them, and re-layouts  3.14 us (4%)
  between operations  1.29 us (2%)
    pallas_call x1, Pallas kernels, local(): pl.pallas_call(functools.partial(kernel, R, C, float((n * R * C) ** (-0.5...  73.3 us
    unnamed x2, local copies, waits for them, and re-layouts  3.14 us

profile of v1, /device:TPU:1, one launch (start us, length us, event | category | flops | bytes accessed | tf_op | source)
XLA Modules:
  0.0 77.7 jit_solution(17229554189375518052)
XLA Ops:
  1.3 73.3 %shard_map.95 = (f32[64,256]{1,0:T(8,128)}, f32[2,16,8,256]{3,2,1,0:T(8,128)}) custom-call(bf16[64,256]{1,0:T(8,128)(2,1)} %feat_ref.1, bf16[64,256]{1,0:T(8,128)(2,1)} %gout_ref.1, s32[64,256]{1,0:T(8,128)} %mask_ref.1, s32[1,64]{1,0:T(1,128)} %bitcast.6, bf16[256,256]{1,0:T(8,128)(2,1)} %w_ref.1, bf16[96,128,128]{2,1,0:T(8,128)(2,1)} %bitcast.4, ...), custom_call_target="tpu_custom_call" | custom-call | tf_op jit(solution)/shard_map/pallas_call | solution.py:241
  74.6 1.5 %copy.13 = f32[64,256]{1,0:T(8,128)} copy(f32[64,256]{1,0:T(8,128)} %get-tuple-element.8) | data formatting | bytes 131072
  76.1 1.7 %copy.14 = f32[256,256]{1,0:T(8,128)} copy(f32[256,256]{1,0:T(8,128)} %bitcast.5) | data formatting | bytes 524288

commit v2 on v1

v2 whole, which is shorter than its diff:
```python
import functools

import jax
import jax.numpy as jnp
from jax import lax
from jax.experimental import pallas as pl
from jax.experimental.pallas import tpu as pltpu
from jax.sharding import PartitionSpec as P

MESH = pl.DeviceIdType.MESH
BF = jnp.bfloat16
F32 = jnp.float32


def kernel(
    R, C, ZH, norm,
    feat_hbm, gout_hbm, mask_hbm, deg_hbm, w_hbm, adj_hbm, slot_ref, count_ref,
    gf_ref, wg_ref,
    feat_v, gout_v, mask_v, deg_v, w_v,
    adj_v, a_dense, inv_v, inv_s, gbuf, fbuf, gt, ptb, pall,
    s1_recv, s2_send, s2_recv, s3_send, s3_recv, own,
    wpart, ra, wb, rb, rc,
    in_sem, adj_sem, inv_sem, gz_ss, gx_ss, g_rs, fy_ss, fz_ss, fc_ss, f_rs,
    s1_ss, s1_rs, s2_ss, s2_rs, s3_ss, s3_rs,
    a_ss, a_rs, b_ss, b_rs, c_ss, c_rs, d_ss, d_rs, e_ss, e_rs,
):
    NY = R // 4
    M = R // 2
    X = C // ZH
    entries, blk = adj_hbm.shape[0], adj_hbm.shape[1]
    n, width = feat_hbm.shape
    row = lax.axis_index("row")
    col = lax.axis_index("col")
    y = row // 4
    z = (row // 2) % 2
    c = row % 2
    m = row // 2
    x = col // ZH
    zh = col % ZH
    sib = (m * 2 + (1 - c), col)
    zdev = (y * 4 + (1 - z) * 2 + c, col)

    def ydev(k):
        return (k * 4 + z * 2 + c, col)

    def rcopy(src, dst, ss, rs, dev):
        return pltpu.make_async_remote_copy(
            src_ref=src, dst_ref=dst, send_sem=ss, recv_sem=rs,
            device_id=dev, device_id_type=MESH,
        )

    def each(lo, hi, body):
        def step(t, u):
            body(t)
            return u

        lax.fori_loop(lo, hi, step, 0)

    loads = [
        pltpu.make_async_copy(s, d, in_sem.at[k])
        for k, (s, d) in enumerate(
            [(gout_hbm, gout_v), (mask_hbm, mask_v), (deg_hbm, deg_v), (feat_hbm, feat_v), (w_hbm, w_v)]
        )
    ]
    for copy in loads:
        copy.start()
    adj_copy = pltpu.make_async_copy(adj_hbm, adj_v.at[pl.ds(0, entries)], adj_sem)
    adj_copy.start()

    bar = pltpu.get_barrier_semaphore()

    def greet(dev):
        pl.semaphore_signal(bar, inc=1, device_id=dev, device_id_type=MESH)

    each(1, ZH, lambda t: greet((row, x * ZH + (zh + t) % ZH)))
    each(1, X, lambda t: greet((row, ((x + t) % X) * ZH + zh)))
    each(1, NY, lambda t: greet(ydev((y + t) % NY)))
    greet(zdev)
    greet(sib)

    for copy in loads[:3]:
        copy.wait()
    scale_row = lax.rsqrt(deg_v[...].astype(F32))
    eye = lax.broadcasted_iota(jnp.int32, (n, n), 0) == lax.broadcasted_iota(jnp.int32, (n, n), 1)
    scale = jnp.sum(jnp.where(eye, jnp.broadcast_to(scale_row, (n, n)), 0.0), axis=1, keepdims=True)
    masked = gout_v[...].astype(F32) * mask_v[...].astype(F32)
    gbuf[col] = (masked * scale).astype(BF)
    loads[3].wait()
    fbuf[row] = (feat_v[...].astype(F32) * scale).astype(BF)

    pl.semaphore_wait(bar, ZH - 1 + X - 1 + NY - 1 + 2)

    def g_copy(slot, ss, dev):
        return rcopy(gbuf.at[slot], gbuf.at[slot], ss, g_rs.at[slot], dev)

    def f_copy(slot, ss, dev):
        return rcopy(fbuf.at[slot], fbuf.at[slot], ss, f_rs.at[slot], dev)

    def to_z(t):
        return g_copy(col, gz_ss.at[t], (row, x * ZH + (zh + t) % ZH))

    def to_x(k, t):
        return g_copy(x * ZH + (zh + k) % ZH, gx_ss.at[k, t], (row, ((x + t) % X) * ZH + zh))

    def f_to_y(t):
        return f_copy(row, fy_ss.at[t], ydev((y + t) % NY))

    def f_to_z(k):
        return f_copy(k * 4 + z * 2 + c, fz_ss.at[k], zdev)

    def f_to_sib(k, zz):
        return f_copy(k * 4 + zz * 2 + c, fc_ss.at[k, zz], sib)

    each(1, ZH, lambda t: to_z(t).start())
    each(1, NY, lambda t: f_to_y(t).start())
    each(1, X, lambda t: to_x(0, t).start())
    f_to_z(y).start()
    f_to_sib(y, z).start()

    lane = lax.broadcasted_iota(jnp.int32, (8, 128), 1)
    live = count_ref[0, 0]

    def invert(b, acc):
        s = jnp.where(b < live, slot_ref[0, b], -1)
        return jnp.where(lane == s, b, acc)

    inv_v[...] = lax.fori_loop(0, entries, invert, jnp.full((8, 128), entries, jnp.int32))
    inv_copy = pltpu.make_async_copy(inv_v, inv_s, inv_sem)
    inv_copy.start()
    adj_v[entries] = jnp.zeros((blk, blk), BF)
    inv_copy.wait()
    adj_copy.wait()

    def fill(k):
        r = k // NY
        q = k % NY
        for h in range(2):
            e = inv_s[0, r * (2 * NY) + q * 2 + h]
            a_dense[q, pl.ds(pl.multiple_of(r * blk, blk), blk), pl.ds(h * blk, blk)] = adj_v[e]

    each(0, C * n // blk * NY, fill)

    def forward_x(k):
        slot = x * ZH + (zh + k) % ZH
        g_copy(slot, gz_ss.at[k], sib).wait_recv()
        each(1, X, lambda t: to_x(k, t).start())

    for k in sorted(range(1, ZH), key=lambda k: min(k, ZH - k)):
        forward_x(k)

    def forward_y(t):
        k = (y + t) % NY
        f_copy(k * 4 + z * 2 + c, fz_ss.at[k], sib).wait_recv()
        f_to_z(k).start()
        f_to_sib(k, z).start()

    each(1, NY, forward_y)

    def forward_z(t):
        k = (y + t) % NY
        f_copy(k * 4 + (1 - z) * 2 + c, fz_ss.at[k], sib).wait_recv()
        f_to_sib(k, 1 - z).start()

    each(0, NY, forward_z)

    def wait_x(t):
        for k in range(ZH):
            g_copy(((x + t) % X) * ZH + k, gz_ss.at[0], sib).wait_recv()

    each(1, X, wait_x)

    def turn(k):
        gt[k] = gbuf[pl.ds(2 * k, 2)].reshape(2 * n, width).T

    each(0, C // 2, turn)
    gtv = jnp.concatenate([gt[k] for k in range(C // 2)], axis=1)

    def s1_copy(q):
        return rcopy(pall.at[q, :, 1 - c], s1_recv.at[q], s1_ss.at[q], s1_rs.at[q], sib)

    def product(t):
        q = (y + 1 + t) % NY
        pt = jnp.dot(gtv, a_dense[q], preferred_element_type=F32)
        pt_hi = pt.astype(BF)
        here = pl.ds(pl.multiple_of(q * 4 * n, 4 * n), 4 * n)
        ptb[0, :, here] = pt_hi
        ptb[1, :, here] = (pt - pt_hi.astype(F32)).astype(BF)
        pall[q] = pt_hi.T.reshape(2, 2, n, width)
        s1_copy(q).start()

    each(0, NY, product)

    def wait_sib(t):
        k = (y + t) % NY
        for zz in range(2):
            f_copy(k * 4 + zz * 2 + 1 - c, fz_ss.at[k], sib).wait_recv()

    each(0, NY, wait_sib)
    fall = fbuf[...].reshape(R * n, width)
    wt = jnp.dot(ptb[0], fall, preferred_element_type=F32) + jnp.dot(ptb[1], fall, preferred_element_type=F32)
    wpart[...] = wt.reshape(wpart.shape)
    a_copy = rcopy(wpart.at[1 - c], ra, a_ss, a_rs, sib)
    a_copy.start()

    def s2_copy(q):
        return rcopy(s2_send.at[q], s2_recv.at[q], s2_ss.at[q], s2_rs.at[q], zdev)

    def stage2(t):
        q = (y + 1 + t) % NY
        s1_copy(q).wait_recv()
        s2_send[q] = (pall[q, 1 - z, c].astype(F32) + s1_recv[q, 1 - z].astype(F32)).astype(BF)
        s2_copy(q).start()

    each(0, NY, stage2)

    a_copy.wait_recv()
    wb[...] = (wpart[c] + ra[...]).astype(BF)

    def b_copy(t):
        peer = (m + t) % M
        return rcopy(wb.at[peer], rb.at[m], b_ss.at[t], b_rs.at[m], (peer * 2 + c, col))

    each(1, M, lambda t: b_copy(t).start())
    rb[m] = wb[m]

    def total3(q):
        s2_copy(q).wait_recv()
        return pall[q, z, c].astype(F32) + s1_recv[q, z].astype(F32) + s2_recv[q].astype(F32)

    def s3_copy(q):
        return rcopy(s3_send.at[q], s3_recv.at[y], s3_ss.at[q], s3_rs.at[y], ydev(q))

    def stage3(t):
        q = (y + 1 + t) % NY
        s3_send[q] = total3(q).astype(BF)
        s3_copy(q).start()

    each(0, NY - 1, stage3)
    own[...] = total3(y)

    def b_wait(t):
        peer = (m + t) % M
        rcopy(wb.at[peer], rb.at[peer], b_ss.at[t], b_rs.at[peer], sib).wait_recv()

    each(1, M, b_wait)
    rc[col] = jnp.sum(rb[...].astype(F32), axis=0).astype(BF)

    def c_copy(t, slot):
        peer = (col + t) % C
        return rcopy(rc.at[slot], rc.at[slot], c_ss.at[t], c_rs.at[slot], (row, peer))

    each(1, C, lambda t: c_copy(t, col).start())

    def collect(t):
        q = (y + t) % NY
        rcopy(s3_send.at[q], s3_recv.at[q], s3_ss.at[q], s3_rs.at[q], sib).wait_recv()
        own[...] += s3_recv[q].astype(F32)

    each(1, NY, collect)

    loads[4].wait()
    pulled = own[...] * scale
    p_hi = pulled.astype(BF)
    p_lo = (pulled - p_hi.astype(F32)).astype(BF)
    over_last = (((1,), (1,)), ((), ()))
    w = w_v[...]
    gf_ref[...] = lax.dot_general(p_hi, w, over_last, preferred_element_type=F32) + lax.dot_general(
        p_lo, w, over_last, preferred_element_type=F32
    )

    each(1, C, lambda t: c_copy(t, (col + t) % C).wait_recv())
    wg_ref[c, m] = (jnp.sum(rc[...].astype(F32), axis=0) * norm).astype(BF)

    def d_copy(t, slot):
        peer = (m + t) % M
        return rcopy(wg_ref.at[c, slot], wg_ref.at[c, slot], d_ss.at[t], d_rs.at[slot], (peer * 2 + c, col))

    each(1, M, lambda t: d_copy(t, m).start())

    each(1, ZH, lambda t: to_z(t).wait_send())
    for k in range(ZH):
        each(1, X, lambda t: to_x(k, t).wait_send())
    each(1, NY, lambda t: f_to_y(t).wait_send())

    def drain(q):
        f_to_z(q).wait_send()
        f_to_sib(q, 0).wait_send()
        f_to_sib(q, 1).wait_send()
        s1_copy(q).wait_send()
        s2_copy(q).wait_send()

    each(0, NY, drain)
    each(1, NY, lambda t: s3_copy((y + t) % NY).wait_send())
    a_copy.wait_send()
    each(1, M, lambda t: b_copy(t).wait_send())
    each(1, C, lambda t: c_copy(t, col).wait_send())

    each(1, M, lambda t: d_copy(t, (m + t) % M).wait())
    rcopy(wg_ref.at[c], wg_ref.at[c], e_ss, e_rs, sib).start()
    rcopy(wg_ref.at[1 - c], wg_ref.at[1 - c], e_ss, e_rs, sib).wait()


def finish(gf_in, wg_in, gf_out, wg_out):
    gf_out[...] = gf_in[...]
    wg_out[...] = wg_in[...].reshape(wg_out.shape).astype(F32).T


def local(ZH, features, grad_out, relu_mask, degree, weight, adjacency, block_slot, block_count):
    R = lax.axis_size("row")
    C = lax.axis_size("col")
    n, width = features.shape
    entries, blk = adjacency.shape[2], adjacency.shape[3]
    NY, M, X = R // 4, R // 2, C // ZH
    part = (2, M, width // R, width)
    dma = pltpu.SemaphoreType.DMA
    vm = pltpu.VMEM
    vspec = pl.BlockSpec(memory_space=pltpu.VMEM)
    sspec = pl.BlockSpec(memory_space=pltpu.SMEM)
    aspec = pl.BlockSpec(memory_space=pl.ANY)
    gf, wg = pl.pallas_call(
        functools.partial(kernel, R, C, ZH, float((n * R * C) ** -0.5)),
        out_shape=(
            jax.ShapeDtypeStruct((n, width), F32),
            jax.ShapeDtypeStruct(part, BF),
        ),
        in_specs=[aspec] * 6 + [sspec, sspec],
        out_specs=(vspec, vspec),
        scratch_shapes=[
            vm((n, width), BF),
            vm((n, width), BF),
            vm((n, width), jnp.int32),
            vm((1, n), jnp.int32),
            vm((width, width), BF),
            vm((entries + 1, blk, blk), BF),
            vm((NY, C * n, 2 * blk), BF),
            vm((8, 128), jnp.int32),
            pltpu.SMEM((8, 128), jnp.int32),
            vm((C, n, width), BF),
            vm((R, n, width), BF),
            vm((C // 2, width, 2 * n), BF),
            vm((2, width, R * n), BF),
            vm((NY, 2, 2, n, width), BF),
            vm((NY, 2, n, width), BF),
            vm((NY, n, width), BF),
            vm((NY, n, width), BF),
            vm((NY, n, width), BF),
            vm((NY, n, width), BF),
            vm((n, width), F32),
            vm(part, F32),
            vm(part[1:], F32),
            vm(part[1:], BF),
            vm(part[1:], BF),
            vm((C,) + part[2:], BF),
            dma((5,)), dma, dma,
            dma((ZH,)), dma((ZH, X)), dma((C,)),
            dma((NY,)), dma((NY,)), dma((NY, 2)), dma((R,)),
            dma((NY,)), dma((NY,)),
            dma((NY,)), dma((NY,)),
            dma((NY,)), dma((NY,)),
            dma, dma,
            dma((M,)), dma((M,)),
            dma((C,)), dma((C,)),
            dma((M,)), dma((M,)),
            dma, dma,
        ],
        compiler_params=pltpu.CompilerParams(
            collective_id=0, has_side_effects=True, vmem_limit_bytes=56 * 1024 * 1024
        ),
    )(
        features, grad_out, relu_mask, degree.reshape(1, n), weight,
        adjacency.reshape(entries, blk, blk), block_slot.reshape(1, entries), block_count,
    )
    return pl.pallas_call(
        finish,
        out_shape=(
            jax.ShapeDtypeStruct((n, width), F32),
            jax.ShapeDtypeStruct((width, width), F32),
        ),
        in_specs=[vspec, vspec],
        out_specs=(vspec, vspec),
    )(gf, wg)


def solution(mesh):
    placed = (
        P(("row", "col"), None),
        P(("row", "col"), None),
        P(("row", "col"), None),
        P(("row", "col")),
        P(),
        P("row", "col", None, None, None),
        P("row", "col", None),
        P("row", "col"),
    )
    inner = min(4, mesh.shape["col"])
    return jax.shard_map(
        functools.partial(local, inner),
        mesh=mesh, in_specs=placed, out_specs=(P(("row", "col"), None), P()), check_vma=False,
    )
```

time: 77.9 us -> 59.4 us (0.76)
  Pallas kernels: 73.3 us -> 57.9 us
  local copies, waits for them, and re-layouts: 3.14 us -> 0 us
    pallas_call x1 -> x2, Pallas kernels: 73.3 us -> 57.9 us  [the longest x1 56.2 us: local(): pl.pallas_call(functools.partial(kernel, R, C, ZH, float((n * R * C) ** (...]
    unnamed x2 -> x0, local copies, waits for them, and re-layouts: 3.14 us -> none
where the time goes in v2:
time: 59.4 us; the launch traced here: 59.2 us
  Pallas kernels  57.9 us (97%)
  between operations  1.29 us (2%)
    pallas_call x1, Pallas kernels, local(): pl.pallas_call(functools.partial(kernel, R, C, ZH, float((n * R * C) ** (...  56.2 us
    pallas_call x1, Pallas kernels, local(): pl.pallas_call(finish, out_shape=(jax.ShapeDtypeStruct((n, width), F32),...  1.75 us

profile of v2, /device:TPU:1, one launch (start us, length us, event | category | flops | bytes accessed | tf_op | source)
XLA Modules:
  0.0 59.2 jit_solution(11785842583984529463)
XLA Ops:
  1.3 56.2 %shard_map.95 = (f32[64,256]{1,0:T(8,128)}, bf16[2,16,8,256]{3,2,1,0:T(8,128)(2,1)}) custom-call(bf16[64,256]{1,0:T(8,128)(2,1)} %feat_hbm.1, bf16[64,256]{1,0:T(8,128)(2,1)} %gout_hbm.1, s32[64,256]{1,0:T(8,128)} %mask_hbm.1, s32[1,64]{1,0:T(1,128)} %bitcast.4, bf16[256,256]{1,0:T(8,128)(2,1)} %w_hbm.1, bf16[96,128,128]{2,1,0:T(8,128)(2,1)} %bitcast.3, ...), custom_call_target="tpu_custom_call" | custom-call | tf_op jit(solution)/shard_map/pallas_call | solution.py:320
  57.5 1.8 %shard_map.96 = (f32[64,256]{1,0:T(8,128)}, f32[256,256]{1,0:T(8,128)}) custom-call(f32[64,256]{1,0:T(8,128)} %get-tuple-element.4.gf_in, bf16[2,16,8,256]{3,2,1,0:T(8,128)(2,1)} %get-tuple-element.5.wg_in), custom_call_target="tpu_custom_call" | custom-call | tf_op jit(solution)/shard_map/pallas_call | solution.py:373

commit v3 on v2

--- a/solution.py
+++ b/solution.py
@@ -49,12 +49,15 @@
             device_id=dev, device_id_type=MESH,
         )
 
-    def each(lo, hi, body):
+    def each(lo, hi, body, unroll=1):
         def step(t, u):
             body(t)
             return u
 
-        lax.fori_loop(lo, hi, step, 0)
+        lax.fori_loop(lo, hi, step, 0, unroll=unroll)
+
+    def off(t, size):
+        return size // 2 + (t // 2) * (2 * (t % 2) - 1)
 
     loads = [
         pltpu.make_async_copy(s, d, in_sem.at[k])
@@ -72,7 +75,7 @@
     def greet(dev):
         pl.semaphore_signal(bar, inc=1, device_id=dev, device_id_type=MESH)
 
-    each(1, ZH, lambda t: greet((row, x * ZH + (zh + t) % ZH)))
+    each(1, ZH, lambda t: greet((row, x * ZH + (zh + off(t, ZH)) % ZH)))
     each(1, X, lambda t: greet((row, ((x + t) % X) * ZH + zh)))
     each(1, NY, lambda t: greet(ydev((y + t) % NY)))
     greet(zdev)
@@ -111,9 +114,9 @@
     def f_to_sib(k, zz):
         return f_copy(k * 4 + zz * 2 + c, fc_ss.at[k, zz], sib)
 
-    each(1, ZH, lambda t: to_z(t).start())
-    each(1, NY, lambda t: f_to_y(t).start())
-    each(1, X, lambda t: to_x(0, t).start())
+    each(1, ZH, lambda t: to_z(off(t, ZH)).start())
+    each(1, NY, lambda t: f_to_y(off(t, NY)).start())
+    each(1, X, lambda t: to_x(0, off(t, X)).start())
     f_to_z(y).start()
     f_to_sib(y, z).start()
 
@@ -143,10 +146,7 @@
     def forward_x(k):
         slot = x * ZH + (zh + k) % ZH
         g_copy(slot, gz_ss.at[k], sib).wait_recv()
-        each(1, X, lambda t: to_x(k, t).start())
-
-    for k in sorted(range(1, ZH), key=lambda k: min(k, ZH - k)):
-        forward_x(k)
+        each(1, X, lambda t: to_x(k, off(t, X)).start())
 
     def forward_y(t):
         k = (y + t) % NY
@@ -154,14 +154,17 @@
         f_to_z(k).start()
         f_to_sib(k, z).start()
 
-    each(1, NY, forward_y)
+    arrivals = [(2 * min(k, ZH - k), 0, k) for k in range(1, ZH)] + [(min(k, NY - k), 1, k) for k in range(1, NY)]
+    for hops, kind, k in sorted(arrivals):
+        if kind:
+            forward_y(k)
+        else:
+            forward_x(k)
 
     def forward_z(t):
-        k = (y + t) % NY
+        k = (y + off(NY - t, NY)) % NY
         f_copy(k * 4 + (1 - z) * 2 + c, fz_ss.at[k], sib).wait_recv()
         f_to_sib(k, 1 - z).start()
-
-    each(0, NY, forward_z)
 
     def wait_x(t):
         for k in range(ZH):
@@ -179,7 +182,8 @@
         return rcopy(pall.at[q, :, 1 - c], s1_recv.at[q], s1_ss.at[q], s1_rs.at[q], sib)
 
     def product(t):
-        q = (y + 1 + t) % NY
+        forward_z(t)
+        q = (y + off(t + 1, NY)) % NY
         pt = jnp.dot(gtv, a_dense[q], preferred_element_type=F32)
         pt_hi = pt.astype(BF)
         here = pl.ds(pl.multiple_of(q * 4 * n, 4 * n), 4 * n)
@@ -188,7 +192,7 @@
         pall[q] = pt_hi.T.reshape(2, 2, n, width)
         s1_copy(q).start()
 
-    each(0, NY, product)
+    each(0, NY, product, 2)
 
     def wait_sib(t):
         k = (y + t) % NY
@@ -206,7 +210,7 @@
         return rcopy(s2_send.at[q], s2_recv.at[q], s2_ss.at[q], s2_rs.at[q], zdev)
 
     def stage2(t):
-        q = (y + 1 + t) % NY
+        q = (y + off(t + 1, NY)) % NY
         s1_copy(q).wait_recv()
         s2_send[q] = (pall[q, 1 - z, c].astype(F32) + s1_recv[q, 1 - z].astype(F32)).astype(BF)
         s2_copy(q).start()
@@ -216,11 +220,14 @@
     a_copy.wait_recv()
     wb[...] = (wpart[c] + ra[...]).astype(BF)
 
+    def row_peer(t):
+        return ((y + off(t // 2 + 1, NY)) % NY) * 2 + (z + 1 - t % 2) % 2
+
     def b_copy(t):
-        peer = (m + t) % M
+        peer = row_peer(t)
         return rcopy(wb.at[peer], rb.at[m], b_ss.at[t], b_rs.at[m], (peer * 2 + c, col))
 
-    each(1, M, lambda t: b_copy(t).start())
+    each(0, M - 1, lambda t: b_copy(t).start())
     rb[m] = wb[m]
 
     def total3(q):
@@ -231,25 +238,28 @@
         return rcopy(s3_send.at[q], s3_recv.at[y], s3_ss.at[q], s3_rs.at[y], ydev(q))
 
     def stage3(t):
-        q = (y + 1 + t) % NY
+        q = (y + off(t, NY)) % NY
         s3_send[q] = total3(q).astype(BF)
         s3_copy(q).start()
 
-    each(0, NY - 1, stage3)
-    own[...] = total3(y)
+    each(1, NY // 2 + 1, stage3)
 
     def b_wait(t):
         peer = (m + t) % M
-        rcopy(wb.at[peer], rb.at[peer], b_ss.at[t], b_rs.at[peer], sib).wait_recv()
+        rcopy(wb.at[peer], rb.at[peer], b_ss.at[t - 1], b_rs.at[peer], sib).wait_recv()
 
     each(1, M, b_wait)
     rc[col] = jnp.sum(rb[...].astype(F32), axis=0).astype(BF)
 
+    def col_peer(t):
+        return ((x + off(t % X + 1, X)) % X) * ZH + (zh + off(t // X + 1, ZH)) % ZH
+
     def c_copy(t, slot):
-        peer = (col + t) % C
-        return rcopy(rc.at[slot], rc.at[slot], c_ss.at[t], c_rs.at[slot], (row, peer))
-
-    each(1, C, lambda t: c_copy(t, col).start())
+        return rcopy(rc.at[slot], rc.at[slot], c_ss.at[t], c_rs.at[slot], (row, col_peer(t)))
+
+    each(0, C - 1, lambda t: c_copy(t, col).start())
+    each(NY // 2 + 1, NY, stage3)
+    own[...] = total3(y)
 
     def collect(t):
         q = (y + t) % NY
@@ -268,14 +278,13 @@
         p_lo, w, over_last, preferred_element_type=F32
     )
 
-    each(1, C, lambda t: c_copy(t, (col + t) % C).wait_recv())
+    each(0, C - 1, lambda t: c_copy(t, col_peer(t)).wait_recv())
     wg_ref[c, m] = (jnp.sum(rc[...].astype(F32), axis=0) * norm).astype(BF)
 
     def d_copy(t, slot):
-        peer = (m + t) % M
-        return rcopy(wg_ref.at[c, slot], wg_ref.at[c, slot], d_ss.at[t], d_rs.at[slot], (peer * 2 + c, col))
-
-    each(1, M, lambda t: d_copy(t, m).start())
+        return rcopy(wg_ref.at[c, slot], wg_ref.at[c, slot], d_ss.at[t], d_rs.at[slot], (row_peer(t) * 2 + c, col))
+
+    each(0, M - 1, lambda t: d_copy(t, m).start())
 
     each(1, ZH, lambda t: to_z(t).wait_send())
     for k in range(ZH):
@@ -292,10 +301,10 @@
     each(0, NY, drain)
     each(1, NY, lambda t: s3_copy((y + t) % NY).wait_send())
     a_copy.wait_send()
-    each(1, M, lambda t: b_copy(t).wait_send())
-    each(1, C, lambda t: c_copy(t, col).wait_send())
-
-    each(1, M, lambda t: d_copy(t, (m + t) % M).wait())
+    each(0, M - 1, lambda t: b_copy(t).wait_send())
+    each(0, C - 1, lambda t: c_copy(t, col).wait_send())
+
+    each(0, M - 1, lambda t: d_copy(t, row_peer(t)).wait())
     rcopy(wg_ref.at[c], wg_ref.at[c], e_ss, e_rs, sib).start()
     rcopy(wg_ref.at[1 - c], wg_ref.at[1 - c], e_ss, e_rs, sib).wait()
 

time: 59.4 us -> 61.5 us (1.035)
  Pallas kernels: 57.9 us -> 60.1 us
    pallas_call x1, Pallas kernels: 56.2 us -> 58.3 us  [local(): pl.pallas_call(functools.partial(kernel, R, C, ZH, float((n * R * C) ** (...]
where the time goes in v3:
time: 61.5 us; the launch traced here: 61.4 us
  Pallas kernels  60.1 us (98%)
  between operations  1.29 us (2%)
    pallas_call x1, Pallas kernels, local(): pl.pallas_call(functools.partial(kernel, R, C, ZH, float((n * R * C) ** (...  58.3 us
    pallas_call x1, Pallas kernels, local(): pl.pallas_call(finish, out_shape=(jax.ShapeDtypeStruct((n, width), F32),...  1.75 us

profile of v3, /device:TPU:1, one launch (start us, length us, event | category | flops | bytes accessed | tf_op | source)
XLA Modules:
  0.0 61.4 jit_solution(17021608001425088082)
XLA Ops:
  1.3 58.3 %shard_map.95 = (f32[64,256]{1,0:T(8,128)}, bf16[2,16,8,256]{3,2,1,0:T(8,128)(2,1)}) custom-call(bf16[64,256]{1,0:T(8,128)(2,1)} %feat_hbm.1, bf16[64,256]{1,0:T(8,128)(2,1)} %gout_hbm.1, s32[64,256]{1,0:T(8,128)} %mask_hbm.1, s32[1,64]{1,0:T(1,128)} %bitcast.4, bf16[256,256]{1,0:T(8,128)(2,1)} %w_hbm.1, bf16[96,128,128]{2,1,0:T(8,128)(2,1)} %bitcast.3, ...), custom_call_target="tpu_custom_call" | custom-call | tf_op jit(solution)/shard_map/pallas_call | solution.py:329
  59.6 1.8 %shard_map.96 = (f32[64,256]{1,0:T(8,128)}, f32[256,256]{1,0:T(8,128)}) custom-call(f32[64,256]{1,0:T(8,128)} %get-tuple-element.4.gf_in, bf16[2,16,8,256]{3,2,1,0:T(8,128)(2,1)} %get-tuple-element.5.wg_in), custom_call_target="tpu_custom_call" | custom-call | tf_op jit(solution)/shard_map/pallas_call | solution.py:382

commit v4 on v3

--- a/solution.py
+++ b/solution.py
@@ -17,10 +17,10 @@
     feat_hbm, gout_hbm, mask_hbm, deg_hbm, w_hbm, adj_hbm, slot_ref, count_ref,
     gf_ref, wg_ref,
     feat_v, gout_v, mask_v, deg_v, w_v,
-    adj_v, a_dense, inv_v, inv_s, gbuf, fbuf, gt, ptb, pall,
-    s1_recv, s2_send, s2_recv, s3_send, s3_recv, own,
+    adj_v, a_dense, inv_v, inv_s, gbuf, fbuf, gt, ft, pall,
+    s1_recv, s_hi, s_lo, s2_recv, s3_send, s3_recv, own,
     wpart, ra, wb, rb, rc,
-    in_sem, adj_sem, inv_sem, gz_ss, gx_ss, g_rs, fy_ss, fz_ss, fc_ss, f_rs,
+    in_sem, adj_sem, inv_sem, gz_ss, gx_ss, g_rs, fy_ss, fz_ss, f_rs,
     s1_ss, s1_rs, s2_ss, s2_rs, s3_ss, s3_rs,
     a_ss, a_rs, b_ss, b_rs, c_ss, c_rs, d_ss, d_rs, e_ss, e_rs,
 ):
@@ -89,7 +89,7 @@
     masked = gout_v[...].astype(F32) * mask_v[...].astype(F32)
     gbuf[col] = (masked * scale).astype(BF)
     loads[3].wait()
-    fbuf[row] = (feat_v[...].astype(F32) * scale).astype(BF)
+    fbuf[m] = (feat_v[...].astype(F32) * scale).astype(BF)
 
     pl.semaphore_wait(bar, ZH - 1 + X - 1 + NY - 1 + 2)
 
@@ -106,19 +106,15 @@
         return g_copy(x * ZH + (zh + k) % ZH, gx_ss.at[k, t], (row, ((x + t) % X) * ZH + zh))
 
     def f_to_y(t):
-        return f_copy(row, fy_ss.at[t], ydev((y + t) % NY))
+        return f_copy(m, fy_ss.at[t], ydev((y + t) % NY))
 
     def f_to_z(k):
-        return f_copy(k * 4 + z * 2 + c, fz_ss.at[k], zdev)
-
-    def f_to_sib(k, zz):
-        return f_copy(k * 4 + zz * 2 + c, fc_ss.at[k, zz], sib)
+        return f_copy(k * 2 + z, fz_ss.at[k], zdev)
 
     each(1, ZH, lambda t: to_z(off(t, ZH)).start())
     each(1, NY, lambda t: f_to_y(off(t, NY)).start())
     each(1, X, lambda t: to_x(0, off(t, X)).start())
     f_to_z(y).start()
-    f_to_sib(y, z).start()
 
     lane = lax.broadcasted_iota(jnp.int32, (8, 128), 1)
     live = count_ref[0, 0]
@@ -150,21 +146,12 @@
 
     def forward_y(t):
         k = (y + t) % NY
-        f_copy(k * 4 + z * 2 + c, fz_ss.at[k], sib).wait_recv()
+        f_copy(k * 2 + z, fz_ss.at[k], sib).wait_recv()
         f_to_z(k).start()
-        f_to_sib(k, z).start()
 
     arrivals = [(2 * min(k, ZH - k), 0, k) for k in range(1, ZH)] + [(min(k, NY - k), 1, k) for k in range(1, NY)]
-    for hops, kind, k in sorted(arrivals):
-        if kind:
-            forward_y(k)
-        else:
-            forward_x(k)
-
-    def forward_z(t):
-        k = (y + off(NY - t, NY)) % NY
-        f_copy(k * 4 + (1 - z) * 2 + c, fz_ss.at[k], sib).wait_recv()
-        f_to_sib(k, 1 - z).start()
+    each(1, ZH, lambda t: forward_x(off(ZH - t, ZH)))
+    each(1, NY, lambda t: forward_y(off(NY - t, NY)))
 
     def wait_x(t):
         for k in range(ZH):
@@ -182,40 +169,39 @@
         return rcopy(pall.at[q, :, 1 - c], s1_recv.at[q], s1_ss.at[q], s1_rs.at[q], sib)
 
     def product(t):
-        forward_z(t)
         q = (y + off(t + 1, NY)) % NY
-        pt = jnp.dot(gtv, a_dense[q], preferred_element_type=F32)
-        pt_hi = pt.astype(BF)
-        here = pl.ds(pl.multiple_of(q * 4 * n, 4 * n), 4 * n)
-        ptb[0, :, here] = pt_hi
-        ptb[1, :, here] = (pt - pt_hi.astype(F32)).astype(BF)
-        pall[q] = pt_hi.T.reshape(2, 2, n, width)
+        pt = jnp.dot(gtv, a_dense[q], preferred_element_type=F32).astype(BF)
+        pall[q] = pt.T.reshape(2, 2, n, width)
         s1_copy(q).start()
 
-    each(0, NY, product, 2)
-
-    def wait_sib(t):
-        k = (y + t) % NY
-        for zz in range(2):
-            f_copy(k * 4 + zz * 2 + 1 - c, fz_ss.at[k], sib).wait_recv()
-
-    each(0, NY, wait_sib)
-    fall = fbuf[...].reshape(R * n, width)
-    wt = jnp.dot(ptb[0], fall, preferred_element_type=F32) + jnp.dot(ptb[1], fall, preferred_element_type=F32)
+    each(0, NY, product)
+
+    each(0, NY, lambda k: f_copy(k * 2 + 1 - z, fz_ss.at[k], sib).wait_recv())
+
+    def turn_f(k):
+        ft[k] = fbuf[pl.ds(2 * k, 2)].reshape(2 * n, width).T
+
+    each(0, NY, turn_f)
+
+    def s2_copy(q):
+        return rcopy(s_hi.at[q, 1 - z], s2_recv.at[q], s2_ss.at[q], s2_rs.at[q], zdev)
+
+    def stage2(t):
+        q = (y + off(t + 1, NY)) % NY
+        s1_copy(q).wait_recv()
+        both = pall[q, :, c].astype(F32) + s1_recv[q].astype(F32)
+        hi = both.astype(BF)
+        s_hi[q] = hi
+        s_lo[q] = (both - hi.astype(F32)).astype(BF)
+        s2_copy(q).start()
+
+    each(0, NY, stage2)
+    ftv = jnp.concatenate([ft[k] for k in range(NY)], axis=1)
+    wt = jnp.dot(ftv, s_hi[...].reshape(M * n, width), preferred_element_type=F32)
+    wt = wt + jnp.dot(ftv, s_lo[...].reshape(M * n, width), preferred_element_type=F32)
     wpart[...] = wt.reshape(wpart.shape)
     a_copy = rcopy(wpart.at[1 - c], ra, a_ss, a_rs, sib)
     a_copy.start()
-
-    def s2_copy(q):
-        return rcopy(s2_send.at[q], s2_recv.at[q], s2_ss.at[q], s2_rs.at[q], zdev)
-
-    def stage2(t):
-        q = (y + off(t + 1, NY)) % NY
-        s1_copy(q).wait_recv()
-        s2_send[q] = (pall[q, 1 - z, c].astype(F32) + s1_recv[q, 1 - z].astype(F32)).astype(BF)
-        s2_copy(q).start()
-
-    each(0, NY, stage2)
 
     a_copy.wait_recv()
     wb[...] = (wpart[c] + ra[...]).astype(BF)
@@ -242,14 +228,15 @@
         s3_send[q] = total3(q).astype(BF)
         s3_copy(q).start()
 
-    each(1, NY // 2 + 1, stage3)
+    each(1, NY, stage3)
+    own[...] = total3(y)
 
     def b_wait(t):
         peer = (m + t) % M
         rcopy(wb.at[peer], rb.at[peer], b_ss.at[t - 1], b_rs.at[peer], sib).wait_recv()
 
     each(1, M, b_wait)
-    rc[col] = jnp.sum(rb[...].astype(F32), axis=0).astype(BF)
+    rc[col] = jnp.sum(rb[...].astype(F32), axis=0)
 
     def col_peer(t):
         return ((x + off(t % X + 1, X)) % X) * ZH + (zh + off(t // X + 1, ZH)) % ZH
@@ -258,8 +245,6 @@
         return rcopy(rc.at[slot], rc.at[slot], c_ss.at[t], c_rs.at[slot], (row, col_peer(t)))
 
     each(0, C - 1, lambda t: c_copy(t, col).start())
-    each(NY // 2 + 1, NY, stage3)
-    own[...] = total3(y)
 
     def collect(t):
         q = (y + t) % NY
@@ -279,7 +264,7 @@
     )
 
     each(0, C - 1, lambda t: c_copy(t, col_peer(t)).wait_recv())
-    wg_ref[c, m] = (jnp.sum(rc[...].astype(F32), axis=0) * norm).astype(BF)
+    wg_ref[c, m] = (jnp.sum(rc[...], axis=0) * norm).astype(BF)
 
     def d_copy(t, slot):
         return rcopy(wg_ref.at[c, slot], wg_ref.at[c, slot], d_ss.at[t], d_rs.at[slot], (row_peer(t) * 2 + c, col))
@@ -293,8 +278,6 @@
 
     def drain(q):
         f_to_z(q).wait_send()
-        f_to_sib(q, 0).wait_send()
-        f_to_sib(q, 1).wait_send()
         s1_copy(q).wait_send()
         s2_copy(q).wait_send()
 
@@ -311,7 +294,7 @@
 
 def finish(gf_in, wg_in, gf_out, wg_out):
     gf_out[...] = gf_in[...]
-    wg_out[...] = wg_in[...].reshape(wg_out.shape).astype(F32).T
+    wg_out[...] = wg_in[...].reshape(wg_out.shape).astype(F32)
 
 
 def local(ZH, features, grad_out, relu_mask, degree, weight, adjacency, block_slot, block_count):
@@ -345,12 +328,13 @@
             vm((8, 128), jnp.int32),
             pltpu.SMEM((8, 128), jnp.int32),
             vm((C, n, width), BF),
-            vm((R, n, width), BF),
+            vm((M, n, width), BF),
             vm((C // 2, width, 2 * n), BF),
-            vm((2, width, R * n), BF),
+            vm((NY, width, 2 * n), BF),
             vm((NY, 2, 2, n, width), BF),
             vm((NY, 2, n, width), BF),
-            vm((NY, n, width), BF),
+            vm((NY, 2, n, width), BF),
+            vm((NY, 2, n, width), BF),
             vm((NY, n, width), BF),
             vm((NY, n, width), BF),
             vm((NY, n, width), BF),
@@ -359,10 +343,10 @@
             vm(part[1:], F32),
             vm(part[1:], BF),
             vm(part[1:], BF),
-            vm((C,) + part[2:], BF),
+            vm((C,) + part[2:], F32),
             dma((5,)), dma, dma,
             dma((ZH,)), dma((ZH, X)), dma((C,)),
-            dma((NY,)), dma((NY,)), dma((NY, 2)), dma((R,)),
+            dma((NY,)), dma((NY,)), dma((M,)),
             dma((NY,)), dma((NY,)),
             dma((NY,)), dma((NY,)),
             dma((NY,)), dma((NY,)),

time: 61.5 us -> 57.4 us (0.933)
  Pallas kernels: 60.1 us -> 56 us
    pallas_call x1, Pallas kernels: 58.3 us -> 54.3 us  [local(): pl.pallas_call(functools.partial(kernel, R, C, ZH, float((n * R * C) ** (...]
where the time goes in v4:
time: 57.4 us; the launch traced here: 57.3 us
  Pallas kernels  56 us (98%)
  between operations  1.29 us (2%)
    pallas_call x1, Pallas kernels, local(): pl.pallas_call(functools.partial(kernel, R, C, ZH, float((n * R * C) ** (...  54.3 us
    pallas_call x1, Pallas kernels, local(): pl.pallas_call(finish, out_shape=(jax.ShapeDtypeStruct((n, width), F32),...  1.67 us

profile of v4, /device:TPU:1, one launch (start us, length us, event | category | flops | bytes accessed | tf_op | source)
XLA Modules:
  0.0 57.3 jit_solution(5153903650740876798)
XLA Ops:
  1.3 54.3 %shard_map.95 = (f32[64,256]{1,0:T(8,128)}, bf16[2,16,8,256]{3,2,1,0:T(8,128)(2,1)}) custom-call(bf16[64,256]{1,0:T(8,128)(2,1)} %feat_hbm.1, bf16[64,256]{1,0:T(8,128)(2,1)} %gout_hbm.1, s32[64,256]{1,0:T(8,128)} %mask_hbm.1, s32[1,64]{1,0:T(1,128)} %bitcast.4, bf16[256,256]{1,0:T(8,128)(2,1)} %w_hbm.1, bf16[96,128,128]{2,1,0:T(8,128)(2,1)} %bitcast.3, ...), custom_call_target="tpu_custom_call" | custom-call | tf_op jit(solution)/shard_map/pallas_call | solution.py:312
  55.6 1.7 %shard_map.96 = (f32[64,256]{1,0:T(8,128)}, f32[256,256]{1,0:T(8,128)}) custom-call(f32[64,256]{1,0:T(8,128)} %get-tuple-element.4.gf_in, bf16[2,16,8,256]{3,2,1,0:T(8,128)(2,1)} %get-tuple-element.5.wg_in), custom_call_target="tpu_custom_call" | custom-call | tf_op jit(solution)/shard_map/pallas_call | solution.py:366

commit v5 on v4

--- a/solution.py
+++ b/solution.py
@@ -10,19 +10,21 @@
 MESH = pl.DeviceIdType.MESH
 BF = jnp.bfloat16
 F32 = jnp.float32
+rem = lax.rem
+div = lax.div
 
 
 def kernel(
     R, C, ZH, norm,
-    feat_hbm, gout_hbm, mask_hbm, deg_hbm, w_hbm, adj_hbm, slot_ref, count_ref,
+    feat_hbm, gout_hbm, mask_hbm, deg_hbm, w_hbm, adj_hbm, slot_hbm, count_hbm,
     gf_ref, wg_ref,
-    feat_v, gout_v, mask_v, deg_v, w_v,
+    feat_v, gout_v, mask_v, deg_v, w_v, slot_ref, count_ref,
     adj_v, a_dense, inv_v, inv_s, gbuf, fbuf, gt, ft, pall,
     s1_recv, s_hi, s_lo, s2_recv, s3_send, s3_recv, own,
     wpart, ra, wb, rb, rc,
     in_sem, adj_sem, inv_sem, gz_ss, gx_ss, g_rs, fy_ss, fz_ss, f_rs,
     s1_ss, s1_rs, s2_ss, s2_rs, s3_ss, s3_rs,
-    a_ss, a_rs, b_ss, b_rs, c_ss, c_rs, d_ss, d_rs, e_ss, e_rs,
+    a_ss, a_rs, b_ss, b_rs, c_ss, c_rs, d_ss, d_rs,
 ):
     NY = R // 4
     M = R // 2
@@ -31,12 +33,12 @@
     n, width = feat_hbm.shape
     row = lax.axis_index("row")
     col = lax.axis_index("col")
-    y = row // 4
-    z = (row // 2) % 2
-    c = row % 2
-    m = row // 2
-    x = col // ZH
-    zh = col % ZH
+    y = div(row, 4)
+    z = rem(div(row, 2), 2)
+    c = rem(row, 2)
+    m = div(row, 2)
+    x = div(col, ZH)
+    zh = rem(col, ZH)
     sib = (m * 2 + (1 - c), col)
     zdev = (y * 4 + (1 - z) * 2 + c, col)
 
@@ -57,29 +59,30 @@
         lax.fori_loop(lo, hi, step, 0, unroll=unroll)
 
     def off(t, size):
-        return size // 2 + (t // 2) * (2 * (t % 2) - 1)
+        return size // 2 + div(t, 2) * (2 * rem(t, 2) - 1)
+
+    bar = pltpu.get_barrier_semaphore()
+
+    def greet(dev):
+        pl.semaphore_signal(bar, inc=1, device_id=dev, device_id_type=MESH)
+
+    each(1, ZH, lambda t: greet((row, x * ZH + rem(zh + off(t, ZH), ZH))))
+    each(1, NY, lambda t: greet(ydev(rem(y + off(t, NY), NY))))
+    each(1, X, lambda t: greet((row, rem(x + off(t, X), X) * ZH + zh)))
+    greet(zdev)
+    greet(sib)
 
     loads = [
         pltpu.make_async_copy(s, d, in_sem.at[k])
         for k, (s, d) in enumerate(
-            [(gout_hbm, gout_v), (mask_hbm, mask_v), (deg_hbm, deg_v), (feat_hbm, feat_v), (w_hbm, w_v)]
+            [(gout_hbm, gout_v), (mask_hbm, mask_v), (deg_hbm, deg_v), (feat_hbm, feat_v), (w_hbm, w_v),
+             (slot_hbm, slot_ref), (count_hbm, count_ref)]
         )
     ]
     for copy in loads:
         copy.start()
     adj_copy = pltpu.make_async_copy(adj_hbm, adj_v.at[pl.ds(0, entries)], adj_sem)
     adj_copy.start()
-
-    bar = pltpu.get_barrier_semaphore()
-
-    def greet(dev):
-        pl.semaphore_signal(bar, inc=1, device_id=dev, device_id_type=MESH)
-
-    each(1, ZH, lambda t: greet((row, x * ZH + (zh + off(t, ZH)) % ZH)))
-    each(1, X, lambda t: greet((row, ((x + t) % X) * ZH + zh)))
-    each(1, NY, lambda t: greet(ydev((y + t) % NY)))
-    greet(zdev)
-    greet(sib)
 
     for copy in loads[:3]:
         copy.wait()
@@ -100,13 +103,13 @@
         return rcopy(fbuf.at[slot], fbuf.at[slot], ss, f_rs.at[slot], dev)
 
     def to_z(t):
-        return g_copy(col, gz_ss.at[t], (row, x * ZH + (zh + t) % ZH))
+        return g_copy(col, gz_ss.at[t], (row, x * ZH + rem(zh + t, ZH)))
 
     def to_x(k, t):
-        return g_copy(x * ZH + (zh + k) % ZH, gx_ss.at[k, t], (row, ((x + t) % X) * ZH + zh))
+        return g_copy(x * ZH + rem(zh + k, ZH), gx_ss.at[k, t], (row, rem(x + t, X) * ZH + zh))
 
     def f_to_y(t):
-        return f_copy(m, fy_ss.at[t], ydev((y + t) % NY))
+        return f_copy(m, fy_ss.at[t], ydev(rem(y + t, NY)))
 
     def f_to_z(k):
         return f_copy(k * 2 + z, fz_ss.at[k], zdev)
@@ -116,6 +119,8 @@
     each(1, X, lambda t: to_x(0, off(t, X)).start())
     f_to_z(y).start()
 
+    loads[5].wait()
+    loads[6].wait()
     lane = lax.broadcasted_iota(jnp.int32, (8, 128), 1)
     live = count_ref[0, 0]
 
@@ -131,8 +136,8 @@
     adj_copy.wait()
 
     def fill(k):
-        r = k // NY
-        q = k % NY
+        r = div(k, NY)
+        q = rem(k, NY)
         for h in range(2):
             e = inv_s[0, r * (2 * NY) + q * 2 + h]
             a_dense[q, pl.ds(pl.multiple_of(r * blk, blk), blk), pl.ds(h * blk, blk)] = adj_v[e]
@@ -140,12 +145,12 @@
     each(0, C * n // blk * NY, fill)
 
     def forward_x(k):
-        slot = x * ZH + (zh + k) % ZH
+        slot = x * ZH + rem(zh + k, ZH)
         g_copy(slot, gz_ss.at[k], sib).wait_recv()
         each(1, X, lambda t: to_x(k, off(t, X)).start())
 
     def forward_y(t):
-        k = (y + t) % NY
+        k = rem(y + t, NY)
         f_copy(k * 2 + z, fz_ss.at[k], sib).wait_recv()
         f_to_z(k).start()
 
@@ -155,7 +160,7 @@
 
     def wait_x(t):
         for k in range(ZH):
-            g_copy(((x + t) % X) * ZH + k, gz_ss.at[0], sib).wait_recv()
+            g_copy(rem(x + t, X) * ZH + k, gz_ss.at[0], sib).wait_recv()
 
     each(1, X, wait_x)
 
@@ -169,7 +174,7 @@
         return rcopy(pall.at[q, :, 1 - c], s1_recv.at[q], s1_ss.at[q], s1_rs.at[q], sib)
 
     def product(t):
-        q = (y + off(t + 1, NY)) % NY
+        q = rem(y + off(t + 1, NY), NY)
         pt = jnp.dot(gtv, a_dense[q], preferred_element_type=F32).astype(BF)
         pall[q] = pt.T.reshape(2, 2, n, width)
         s1_copy(q).start()
@@ -187,7 +192,7 @@
         return rcopy(s_hi.at[q, 1 - z], s2_recv.at[q], s2_ss.at[q], s2_rs.at[q], zdev)
 
     def stage2(t):
-        q = (y + off(t + 1, NY)) % NY
+        q = rem(y + off(t + 1, NY), NY)
         s1_copy(q).wait_recv()
         both = pall[q, :, c].astype(F32) + s1_recv[q].astype(F32)
         hi = both.astype(BF)
@@ -207,7 +212,7 @@
     wb[...] = (wpart[c] + ra[...]).astype(BF)
 
     def row_peer(t):
-        return ((y + off(t // 2 + 1, NY)) % NY) * 2 + (z + 1 - t % 2) % 2
+        return (rem(y + off(div(t, 2) + 1, NY), NY)) * 2 + rem(z + 1 - rem(t, 2), 2)
 
     def b_copy(t):
         peer = row_peer(t)
@@ -224,7 +229,7 @@
         return rcopy(s3_send.at[q], s3_recv.at[y], s3_ss.at[q], s3_rs.at[y], ydev(q))
 
     def stage3(t):
-        q = (y + off(t, NY)) % NY
+        q = rem(y + off(t, NY), NY)
         s3_send[q] = total3(q).astype(BF)
         s3_copy(q).start()
 
@@ -232,14 +237,14 @@
     own[...] = total3(y)
 
     def b_wait(t):
-        peer = (m + t) % M
+        peer = rem(m + t, M)
         rcopy(wb.at[peer], rb.at[peer], b_ss.at[t - 1], b_rs.at[peer], sib).wait_recv()
 
     each(1, M, b_wait)
     rc[col] = jnp.sum(rb[...].astype(F32), axis=0)
 
     def col_peer(t):
-        return ((x + off(t % X + 1, X)) % X) * ZH + (zh + off(t // X + 1, ZH)) % ZH
+        return ((x + off(rem(t, X) + 1, X)) % X) * ZH + rem(zh + off(div(t, X) + 1, ZH), ZH)
 
     def c_copy(t, slot):
         return rcopy(rc.at[slot], rc.at[slot], c_ss.at[t], c_rs.at[slot], (row, col_peer(t)))
@@ -247,7 +252,7 @@
     each(0, C - 1, lambda t: c_copy(t, col).start())
 
     def collect(t):
-        q = (y + t) % NY
+        q = rem(y + t, NY)
         rcopy(s3_send.at[q], s3_recv.at[q], s3_ss.at[q], s3_rs.at[q], sib).wait_recv()
         own[...] += s3_recv[q].astype(F32)
 
@@ -266,10 +271,17 @@
     each(0, C - 1, lambda t: c_copy(t, col_peer(t)).wait_recv())
     wg_ref[c, m] = (jnp.sum(rc[...], axis=0) * norm).astype(BF)
 
-    def d_copy(t, slot):
-        return rcopy(wg_ref.at[c, slot], wg_ref.at[c, slot], d_ss.at[t], d_rs.at[slot], (row_peer(t) * 2 + c, col))
-
-    each(0, M - 1, lambda t: d_copy(t, m).start())
+    def d_copy(t, slot, core):
+        return rcopy(wg_ref.at[c, slot], wg_ref.at[c, slot], d_ss.at[core, t], d_rs.at[c, slot], (row_peer(t) * 2 + core, col))
+
+    def d_start(t):
+        d_copy(t, m, 1 - c).start()
+
+        @pl.when(t < M - 1)
+        def _():
+            d_copy(t, m, c).start()
+
+    each(0, M, d_start)
 
     each(1, ZH, lambda t: to_z(t).wait_send())
     for k in range(ZH):
@@ -282,14 +294,21 @@
         s2_copy(q).wait_send()
 
     each(0, NY, drain)
-    each(1, NY, lambda t: s3_copy((y + t) % NY).wait_send())
+    each(1, NY, lambda t: s3_copy(rem(y + t, NY)).wait_send())
     a_copy.wait_send()
     each(0, M - 1, lambda t: b_copy(t).wait_send())
     each(0, C - 1, lambda t: c_copy(t, col).wait_send())
 
-    each(0, M - 1, lambda t: d_copy(t, row_peer(t)).wait())
-    rcopy(wg_ref.at[c], wg_ref.at[c], e_ss, e_rs, sib).start()
-    rcopy(wg_ref.at[1 - c], wg_ref.at[1 - c], e_ss, e_rs, sib).wait()
+    def d_wait(t):
+        d_copy(t, m, 1 - c).wait_send()
+        rcopy(wg_ref.at[1 - c, t], wg_ref.at[1 - c, t], d_ss.at[0, t], d_rs.at[1 - c, t], sib).wait_recv()
+
+        @pl.when(t < M - 1)
+        def _():
+            d_copy(t, m, c).wait_send()
+            d_copy(t, row_peer(t), c).wait_recv()
+
+    each(0, M, d_wait)
 
 
 def finish(gf_in, wg_in, gf_out, wg_out):
@@ -307,15 +326,14 @@
     dma = pltpu.SemaphoreType.DMA
     vm = pltpu.VMEM
     vspec = pl.BlockSpec(memory_space=pltpu.VMEM)
-    sspec = pl.BlockSpec(memory_space=pltpu.SMEM)
-    aspec = pl.BlockSpec(memory_space=pl.ANY)
+    aspec = pl.BlockSpec(memory_space=pltpu.HBM)
     gf, wg = pl.pallas_call(
         functools.partial(kernel, R, C, ZH, float((n * R * C) ** -0.5)),
         out_shape=(
             jax.ShapeDtypeStruct((n, width), F32),
             jax.ShapeDtypeStruct(part, BF),
         ),
-        in_specs=[aspec] * 6 + [sspec, sspec],
+        in_specs=[aspec] * 8,
         out_specs=(vspec, vspec),
         scratch_shapes=[
             vm((n, width), BF),
@@ -323,6 +341,8 @@
             vm((n, width), jnp.int32),
             vm((1, n), jnp.int32),
             vm((width, width), BF),
+            pltpu.SMEM((1, entries), jnp.int32),
+            pltpu.SMEM((1, 1), jnp.int32),
             vm((entries + 1, blk, blk), BF),
             vm((NY, C * n, 2 * blk), BF),
             vm((8, 128), jnp.int32),
@@ -344,7 +364,7 @@
             vm(part[1:], BF),
             vm(part[1:], BF),
             vm((C,) + part[2:], F32),
-            dma((5,)), dma, dma,
+            dma((7,)), dma, dma,
             dma((ZH,)), dma((ZH, X)), dma((C,)),
             dma((NY,)), dma((NY,)), dma((M,)),
             dma((NY,)), dma((NY,)),
@@ -353,8 +373,7 @@
             dma, dma,
             dma((M,)), dma((M,)),
             dma((C,)), dma((C,)),
-            dma((M,)), dma((M,)),
-            dma, dma,
+            dma((2, M)), dma((2, M)),
         ],
         compiler_params=pltpu.CompilerParams(
             collective_id=0, has_side_effects=True, vmem_limit_bytes=56 * 1024 * 1024

time: 57.4 us -> 55.4 us (0.965)
  Pallas kernels: 56 us -> 53.9 us
    pallas_call x1, Pallas kernels: 54.3 us -> 52.2 us  [local(): pl.pallas_call(functools.partial(kernel, R, C, ZH, float((n * R * C) ** (...]
where the time goes in v5:
time: 55.4 us; the launch traced here: 55.2 us
  Pallas kernels  53.9 us (97%)
  between operations  1.29 us (2%)
    pallas_call x1, Pallas kernels, local(): pl.pallas_call(functools.partial(kernel, R, C, ZH, float((n * R * C) ** (...  52.2 us
    pallas_call x1, Pallas kernels, local(): pl.pallas_call(finish, out_shape=(jax.ShapeDtypeStruct((n, width), F32),...  1.67 us

profile of v5, /device:TPU:1, one launch (start us, length us, event | category | flops | bytes accessed | tf_op | source)
XLA Modules:
  0.0 55.2 jit_solution(15467223323034690419)
XLA Ops:
  1.3 52.2 %shard_map.95 = (f32[64,256]{1,0:T(8,128)}, bf16[2,16,8,256]{3,2,1,0:T(8,128)(2,1)}) custom-call(bf16[64,256]{1,0:T(8,128)(2,1)} %feat_hbm.1, bf16[64,256]{1,0:T(8,128)(2,1)} %gout_hbm.1, s32[64,256]{1,0:T(8,128)} %mask_hbm.1, s32[1,64]{1,0:T(1,128)} %bitcast.4, bf16[256,256]{1,0:T(8,128)(2,1)} %w_hbm.1, bf16[96,128,128]{2,1,0:T(8,128)(2,1)} %bitcast.3, ...), custom_call_target="tpu_custom_call" | custom-call | tf_op jit(solution)/shard_map/pallas_call | solution.py:330
  53.5 1.7 %shard_map.96 = (f32[64,256]{1,0:T(8,128)}, f32[256,256]{1,0:T(8,128)}) custom-call(f32[64,256]{1,0:T(8,128)} %get-tuple-element.4.gf_in, bf16[2,16,8,256]{3,2,1,0:T(8,128)(2,1)} %get-tuple-element.5.wg_in), custom_call_target="tpu_custom_call" | custom-call | tf_op jit(solution)/shard_map/pallas_call | solution.py:385

commit v6 on v5

--- a/solution.py
+++ b/solution.py
@@ -159,15 +159,18 @@
     each(1, NY, lambda t: forward_y(off(NY - t, NY)))
 
     def wait_x(t):
-        for k in range(ZH):
-            g_copy(rem(x + t, X) * ZH + k, gz_ss.at[0], sib).wait_recv()
-
-    each(1, X, wait_x)
-
-    def turn(k):
-        gt[k] = gbuf[pl.ds(2 * k, 2)].reshape(2 * n, width).T
-
-    each(0, C // 2, turn)
+        there = rem(x + t, X)
+
+        @pl.when(t > 0)
+        def _():
+            for k in range(ZH):
+                g_copy(there * ZH + k, gz_ss.at[0], sib).wait_recv()
+
+        for k in range(ZH // 2):
+            pair = there * (ZH // 2) + k
+            gt[pair] = gbuf[pl.ds(2 * pair, 2)].reshape(2 * n, width).T
+
+    each(0, X, wait_x)
     gtv = jnp.concatenate([gt[k] for k in range(C // 2)], axis=1)
 
     def s1_copy(q):
@@ -233,8 +236,7 @@
         s3_send[q] = total3(q).astype(BF)
         s3_copy(q).start()
 
-    each(1, NY, stage3)
-    own[...] = total3(y)
+    each(1, NY // 2 + 1, stage3)
 
     def b_wait(t):
         peer = rem(m + t, M)
@@ -250,6 +252,8 @@
         return rcopy(rc.at[slot], rc.at[slot], c_ss.at[t], c_rs.at[slot], (row, col_peer(t)))
 
     each(0, C - 1, lambda t: c_copy(t, col).start())
+    each(NY // 2 + 1, NY, stage3)
+    own[...] = total3(y)
 
     def collect(t):
         q = rem(y + t, NY)

time: 55.4 us -> 55.1 us (level)
  no operation moved by 1% of the time
where the time goes in v6:
time: 55.1 us; the launch traced here: 54.9 us
  Pallas kernels  53.6 us (97%)
  between operations  1.29 us (2%)
    pallas_call x1, Pallas kernels, local(): pl.pallas_call(functools.partial(kernel, R, C, ZH, float((n * R * C) ** (...  52 us
    pallas_call x1, Pallas kernels, local(): pl.pallas_call(finish, out_shape=(jax.ShapeDtypeStruct((n, width), F32),...  1.67 us

profile of v6, /device:TPU:1, one launch (start us, length us, event | category | flops | bytes accessed | tf_op | source)
XLA Modules:
  0.0 54.9 jit_solution(8824914611939022789)
XLA Ops:
  1.3 52.0 %shard_map.95 = (f32[64,256]{1,0:T(8,128)}, bf16[2,16,8,256]{3,2,1,0:T(8,128)(2,1)}) custom-call(bf16[64,256]{1,0:T(8,128)(2,1)} %feat_hbm.1, bf16[64,256]{1,0:T(8,128)(2,1)} %gout_hbm.1, s32[64,256]{1,0:T(8,128)} %mask_hbm.1, s32[1,64]{1,0:T(1,128)} %bitcast.4, bf16[256,256]{1,0:T(8,128)(2,1)} %w_hbm.1, bf16[96,128,128]{2,1,0:T(8,128)(2,1)} %bitcast.3, ...), custom_call_target="tpu_custom_call" | custom-call | tf_op jit(solution)/shard_map/pallas_call | solution.py:334
  53.2 1.7 %shard_map.96 = (f32[64,256]{1,0:T(8,128)}, f32[256,256]{1,0:T(8,128)}) custom-call(f32[64,256]{1,0:T(8,128)} %get-tuple-element.4.gf_in, bf16[2,16,8,256]{3,2,1,0:T(8,128)(2,1)} %get-tuple-element.5.wg_in), custom_call_target="tpu_custom_call" | custom-call | tf_op jit(solution)/shard_map/pallas_call | solution.py:389

commit v7 on v6

--- a/solution.py
+++ b/solution.py
@@ -236,7 +236,7 @@
         s3_send[q] = total3(q).astype(BF)
         s3_copy(q).start()
 
-    each(1, NY // 2 + 1, stage3)
+    each(1, NY // 4 + 1, stage3)
 
     def b_wait(t):
         peer = rem(m + t, M)
@@ -252,7 +252,7 @@
         return rcopy(rc.at[slot], rc.at[slot], c_ss.at[t], c_rs.at[slot], (row, col_peer(t)))
 
     each(0, C - 1, lambda t: c_copy(t, col).start())
-    each(NY // 2 + 1, NY, stage3)
+    each(NY // 4 + 1, NY, stage3)
     own[...] = total3(y)
 
     def collect(t):

time: 55.1 us -> 56.1 us (1.018)
  Pallas kernels: 53.6 us -> 54.6 us
    pallas_call x1, Pallas kernels: 52 us -> 53 us  [local(): pl.pallas_call(functools.partial(kernel, R, C, ZH, float((n * R * C) ** (...]
where the time goes in v7:
time: 56.1 us; the launch traced here: 55.9 us
  Pallas kernels  54.6 us (97%)
  between operations  1.29 us (2%)
    pallas_call x1, Pallas kernels, local(): pl.pallas_call(functools.partial(kernel, R, C, ZH, float((n * R * C) ** (...  53 us
    pallas_call x1, Pallas kernels, local(): pl.pallas_call(finish, out_shape=(jax.ShapeDtypeStruct((n, width), F32),...  1.67 us

profile of v7, /device:TPU:1, one launch (start us, length us, event | category | flops | bytes accessed | tf_op | source)
XLA Modules:
  0.0 55.9 jit_solution(15845267887681367468)
XLA Ops:
  1.3 53.0 %shard_map.95 = (f32[64,256]{1,0:T(8,128)}, bf16[2,16,8,256]{3,2,1,0:T(8,128)(2,1)}) custom-call(bf16[64,256]{1,0:T(8,128)(2,1)} %feat_hbm.1, bf16[64,256]{1,0:T(8,128)(2,1)} %gout_hbm.1, s32[64,256]{1,0:T(8,128)} %mask_hbm.1, s32[1,64]{1,0:T(1,128)} %bitcast.4, bf16[256,256]{1,0:T(8,128)(2,1)} %w_hbm.1, bf16[96,128,128]{2,1,0:T(8,128)(2,1)} %bitcast.3, ...), custom_call_target="tpu_custom_call" | custom-call | tf_op jit(solution)/shard_map/pallas_call | solution.py:334
  54.2 1.7 %shard_map.96 = (f32[64,256]{1,0:T(8,128)}, f32[256,256]{1,0:T(8,128)}) custom-call(f32[64,256]{1,0:T(8,128)} %get-tuple-element.4.gf_in, bf16[2,16,8,256]{3,2,1,0:T(8,128)(2,1)} %get-tuple-element.5.wg_in), custom_call_target="tpu_custom_call" | custom-call | tf_op jit(solution)/shard_map/pallas_call | solution.py:389
